TPU v7x, 512 devices: a whole 4x8x8 slice. The times are simulated.
512 devices in a mesh: row: 16 (over y, core), col: 32 (over x, z).
Axes of the slice: x: 4, y: 8, z: 8, core: 2. Of those that a mesh axis runs over, the one named last changes fastest.
Arguments:
- demand: bfloat16 [196608, 128], P(('row', 'col')), may hold values from -6 to 6
- tile_data: bfloat16 [16, 32, 128, 128, 128], P('row', 'col'), may hold values from -0.078125 to 0.078125
- tile_row: int32 [16, 32, 128], P('row', 'col'), may hold values from 0 to 48, as said below
- tile_col: int32 [16, 32, 128], P('row', 'col'), may hold values from 0 to 95, as said below
Outputs:
- leontief: bfloat16 [196608, 128], P(('row', 'col'))
Inputs may be any that keep to these rules, and one draw needn't show every extreme that they name: `tile_row`: the value 16 * 3 marks an empty slot. In every index pair the live slots come first and number at least 42; in every draw some index pair has all 128 slots live. Two slots may name the same tile position; their tiles then add. `tile_col`: empty slots carry a column too, which is ignored.
All inputs are finite; a program needn't handle non-finite values.
Results may differ from a plain program's by a relative error of at most 0.018.
Values may be sent and summed in bfloat16 or wider, within the bound.
No kernel may reach another device: no remote copies, remote signals or barrier semaphores. Data moves between devices by JAX's collectives and lax.ppermute only.
A program may use at most 64 MiB of HBM per device.

v0:
```python
import jax
import jax.numpy as jnp
from jax import lax
from jax.sharding import Mesh
from jax.sharding import PartitionSpec as P

COL = ("col_0", "col_1")
ROW_COL = ("row", "col_0", "col_1")


def in_order(blocks, dim):
    shape = list(blocks.shape[1:])
    shape[dim] *= blocks.shape[0]
    return jnp.moveaxis(blocks, 0, dim).reshape(shape)


def gather_in_order(array, axes, order):
    blocks = array[None]
    for k in order:
        blocks = lax.all_gather(blocks, axes[k], axis=0, tiled=True)
    held = [lax.axis_size(axes[k]) for k in reversed(order)]
    blocks = blocks.reshape(*held, *array.shape)
    turned = sorted(range(len(order)), key=lambda place: order[len(order) - 1 - place])
    return blocks.transpose(*turned, *range(len(order), blocks.ndim)).reshape(-1, *array.shape)


def gather_axes(array, axes, order, dim):
    return in_order(gather_in_order(array, axes, order), dim)


def cut_along(array, dim, devices):
    shape = array.shape
    blocks = array.reshape(*shape[:dim], devices, shape[dim] // devices, *shape[dim + 1 :])
    return jnp.moveaxis(blocks, dim, 0)


def summed_on_arrival(array, axis, dim):
    blocks = cut_along(array, dim, lax.axis_size(axis))
    arrived = lax.all_to_all(blocks, axis, split_axis=0, concat_axis=0, tiled=True)
    return arrived.astype(jnp.float32).sum(axis=0)


def multiply(panel_piece, tile_block, slot_rows, slot_cols):
    edge = tile_block.shape[-1]
    columns = panel_piece.shape[1]
    slot_count = tile_block.shape[0]
    local_rows = lax.axis_size("row") * (panel_piece.shape[0] // edge)
    gathered = gather_axes(panel_piece, COL, (0, 1), 0)
    blocks = gathered.reshape(-1, edge, columns)
    picked = jnp.take(blocks, slot_cols, axis=0)
    products = jnp.einsum("stk,skc->stc", tile_block, picked, preferred_element_type=jnp.float32)
    products = products.reshape(slot_count, -1)
    upper = products.astype(jnp.bfloat16)
    lower = (products - upper.astype(jnp.float32)).astype(jnp.bfloat16)
    targets = jnp.arange(local_rows, dtype=jnp.int32)
    onehot = (slot_rows[None, :] == targets[:, None]).astype(jnp.bfloat16)
    partial_value = jnp.dot(onehot, upper, preferred_element_type=jnp.float32)
    partial_value = partial_value + jnp.dot(onehot, lower, preferred_element_type=jnp.float32)
    partial_value = lax.optimization_barrier(partial_value.astype(jnp.bfloat16)).astype(jnp.float32)
    partial_value = partial_value.reshape(local_rows * edge, columns)
    summed = summed_on_arrival(partial_value.astype(jnp.bfloat16), "row", 0)
    return summed.astype(jnp.bfloat16)


def body(demand, tile_data, tile_row, tile_col):
    tile_block = tile_data[0, 0]
    slot_rows = tile_row[0, 0]
    slot_cols = tile_col[0, 0]
    first_term = multiply(demand, tile_block, slot_rows, slot_cols)
    second_term = multiply(first_term, tile_block, slot_rows, slot_cols)
    summed = (
        demand.astype(jnp.float32)
        + first_term.astype(jnp.float32)
        + second_term.astype(jnp.float32)
    )
    return summed.astype(jnp.bfloat16)


def solution(mesh):
    torus = Mesh(mesh.devices.reshape(mesh.shape["row"], 4, 8), ("row", "col_0", "col_1"))
    return jax.shard_map(
        body,
        mesh=torus,
        in_specs=(
            P(ROW_COL, None),
            P("row", COL, None, None, None),
            P("row", COL, None),
            P("row", COL, None),
        ),
        out_specs=P(ROW_COL, None),
        check_vma=False,
    )
```

profile of v0, /device:TPU:1, one launch (start us, length us, event | category | flops | bytes accessed | tf_op | source)
XLA Modules:
  0.0 296.3 jit_solution(10210878075228454600)
XLA Ops:
  6.5 0.0 all-gather.5.cloned.1.call-start
  6.5 13.0 %all-gather = bf16[1536,128]{1,0:T(8,128)(2,1)} all-gather(bf16[384,128]{1,0:T(8,128)(2,1)} %param.6), channel_id=2, replica_groups=mesh['row'=16,'col_0'=4,'col_1'=8] {'col_0'}, dimensions={0}, use_global_device_ids=true | all-gather | bytes 491520 | tf_op jit(solution)/shard_map/all_gather | solution.py:20
  19.5 0.0 all-gather.5.cloned.1.call-update
  19.5 0.0 all-gather.7.cloned.1.call-start
  19.6 0.7 compare_select_fusion
  20.2 0.7 compare_and_fusion
  20.9 52.9 %all-gather.5.cloned.1.call-done = bf16[32,384,128]{2,1,0:T(8,128)(2,1)} async-done(((bf16[4,384,128]{2,1,0:T(8,128)(2,1)}), bf16[32,384,128]{2,1,0:T(8,128)(2,1)}) %all-gather.5.cloned.1.call-update) | async-done | bytes 3145744 | tf_op jit(solution)/shard_map/all_gather | solution.py:20
  73.8 2.1 copy.15
  76.0 3.0 %gather_fusion = bf16[128,128,128]{2,1,0:T(8,128)(2,1)} fusion(bf16[96,128,128]{2,1,0:T(8,128)(2,1)S(1)} %bitcast.45, s32[1024]{0:T(1024)S(1)} %pad_clamp_fusion), kind=kCustom, calls=%fused_computation.clone | custom fusion | bytes 8389120 | tf_op jit(solution)/shard_map/jit(_take)/gather | solution.py:50
  79.0 9.9 %fusion.12 = f32[128,128,128]{1,2,0:T(8,128)} fusion(bf16[1,1,128,128,128]{4,3,2,1,0:T(8,128)(2,1)} %param.7, bf16[128,128,128]{2,1,0:T(8,128)(2,1)} %gather_fusion, pred[128]{0:T(512)(128)(4,1)S(1)} %compare_and_fusion), kind=kOutput, calls=%fused_computation.20 | convolution fusion | flops 538968064 | bytes 16777344 | tf_op jit(solution)/shard_map/stk,skc->stc/dot_general | solution.py:51
  88.9 9.4 %copy.17 = f32[128,128,128]{0,2,1:T(8,128)} copy(f32[128,128,128]{1,2,0:T(8,128)} %fusion.12) | data formatting | bytes 16777216 | tf_op jit(solution)/shard_map/stk,skc->stc/dot_general | solution.py:51
  98.3 0.0 copy-start.1
  98.3 4.0 %fusion.3 = (bf16[128,16384]{0,1:T(8,128)(2,1)S(1)}, bf16[128,16384]{0,1:T(8,128)(2,1)S(1)}) fusion(f32[128,128,128]{0,2,1:T(8,128)} %copy.17), kind=kLoop, calls=%fused_computation.11 | loop fusion | flops 8388608 | bytes 16777216 | tf_op jit(solution)/shard_map/convert_element_type | solution.py:54
  102.3 0.0 copy-done.1
  102.4 1.5 fusion.25
  103.9 1.5 fusion
  105.5 0.8 convert_element_type.59
  106.2 47.0 %all_to_all.10 = bf16[16,384,128]{2,1,0:T(8,128)(2,1)S(1)} all-to-all(bf16[16,384,128]{2,1,0:T(8,128)(2,1)S(1)} %convert_element_type.59), channel_id=1, replica_groups=mesh['row'=16,'col_0'=4,'col_1'=8] {'row'}, dimensions={0} | all-to-all | bytes 3145728 | tf_op jit(solution)/shard_map/all_to_all | solution.py:39
  153.2 0.2 reduce_sum.24
  153.4 11.9 %all-gather.1 = bf16[1536,128]{1,0:T(8,128)(2,1)} all-gather(bf16[384,128]{1,0:T(8,128)(2,1)S(1)} %reduce_sum.24), channel_id=3, replica_groups=mesh['row'=16,'col_0'=4,'col_1'=8] {'col_0'}, dimensions={0}, use_global_device_ids=true | all-gather | bytes 491520 | tf_op jit(solution)/shard_map/all_gather | solution.py:20
  165.4 0.0 all-gather.7.cloned.1.call-update
  165.4 43.8 %all-gather.7.cloned.1.call-done = bf16[32,384,128]{2,1,0:T(8,128)(2,1)} async-done(((bf16[4,384,128]{2,1,0:T(8,128)(2,1)}), bf16[32,384,128]{2,1,0:T(8,128)(2,1)}) %all-gather.7.cloned.1.call-update) | async-done | bytes 3145744 | tf_op jit(solution)/shard_map/all_gather | solution.py:20
  209.2 2.1 copy.18
  211.3 3.0 %gather_fusion.1 = bf16[128,128,128]{2,1,0:T(8,128)(2,1)} fusion(bf16[96,128,128]{2,1,0:T(8,128)(2,1)S(1)} %bitcast.44, s32[1024]{0:T(1024)S(1)} %pad_clamp_fusion), kind=kCustom, calls=%fused_computation.1.clone | custom fusion | bytes 8389120 | tf_op jit(solution)/shard_map/jit(_take)/gather | solution.py:50
  214.4 9.9 %fusion.17 = f32[128,128,128]{1,2,0:T(8,128)} fusion(bf16[1,1,128,128,128]{4,3,2,1,0:T(8,128)(2,1)} %param.7, bf16[128,128,128]{2,1,0:T(8,128)(2,1)} %gather_fusion.1, pred[128]{0:T(512)(128)(4,1)S(1)} %compare_and_fusion), kind=kOutput, calls=%fused_computation.21 | convolution fusion | flops 538968064 | bytes 16777344 | tf_op jit(solution)/shard_map/stk,skc->stc/dot_general | solution.py:51
  224.3 9.4 %copy.20 = f32[128,128,128]{0,2,1:T(8,128)} copy(f32[128,128,128]{1,2,0:T(8,128)} %fusion.17) | data formatting | bytes 16777216 | tf_op jit(solution)/shard_map/stk,skc->stc/dot_general | solution.py:51
  233.7 4.0 %fusion.2 = (bf16[128,16384]{0,1:T(8,128)(2,1)S(1)}, bf16[128,16384]{0,1:T(8,128)(2,1)S(1)}) fusion(f32[128,128,128]{0,2,1:T(8,128)} %copy.20), kind=kLoop, calls=%fused_computation.8 | loop fusion | flops 8388608 | bytes 16777216 | tf_op jit(solution)/shard_map/convert_element_type | solution.py:54
  237.7 1.5 fusion.24
  239.3 1.5 fusion.1
  240.8 0.0 copy-start
  240.8 0.8 convert_element_type.65
  241.6 47.0 %all_to_all.11 = bf16[16,384,128]{2,1,0:T(8,128)(2,1)S(1)} all-to-all(bf16[16,384,128]{2,1,0:T(8,128)(2,1)S(1)} %convert_element_type.65), channel_id=1, replica_groups=mesh['row'=16,'col_0'=4,'col_1'=8] {'row'}, dimensions={0} | all-to-all | bytes 3145728 | tf_op jit(solution)/shard_map/all_to_all | solution.py:39
  288.6 0.2 reduce_sum.25
  288.8 0.0 copy-done
  288.8 0.7 add_convert_fusion
  (1 shorter events, 0.0 us)
Async XLA Ops:
  6.5 67.3 %all-gather.5.cloned.1.call-start = ((), (), s32[]{:S(2)}) async-start(), calls=%async_computation.2 | async-start | bytes 3538944 | tf_op jit(solution)/shard_map/all_gather | solution.py:20
  19.5 189.7 %all-gather.7.cloned.1.call-start = ((), (), s32[]{:S(2)}) async-start(), calls=%async_computation.3 | async-start | bytes 3538944 | tf_op jit(solution)/shard_map/all_gather | solution.py:20
  98.3 4.0 %copy-start.1 = (s32[1,1,128]{2,1,0:T(1,128)S(1)}, s32[1,1,128]{2,1,0:T(1,128)}, u32[]{:S(2)}) copy-start(s32[1,1,128]{2,1,0:T(1,128)} %param.8) | copy-start | bytes 1540
  240.8 48.0 %copy-start = (bf16[384,128]{1,0:T(8,128)(2,1)S(1)}, bf16[384,128]{1,0:T(8,128)(2,1)}, u32[]{:S(2)}) copy-start(bf16[384,128]{1,0:T(8,128)(2,1)} %param.6) | copy-start | bytes 294916
Sparse Core Ops, SparseCore 0:
  19.6 54.1 all-gather.4
  165.5 43.6 all-gather.6
where the time goes:
time: 297 us; the launch traced here: 296 us
  blocking collectives  119 us (40%)
  waiting for transfers between devices  96.8 us (33%)
  local copies, waits for them, and re-layouts  30.6 us (10%)
  matrix products  26 us (9%)
  between operations  13.5 us (5%)
  other arithmetic  10.5 us (4%)
    all_gather x2, waiting for transfers between devices, gather_in_order(): blocks = lax.all_gather(blocks, axes[k], axis=0, tiled=True)  96.8 us
    all_to_all x2, blocking collectives, summed_on_arrival(): lax.all_to_all(blocks, axis, split_axis=0, concat_axis=0, tiled=True)  94 us
    all_gather x2, blocking collectives, gather_in_order(): blocks = lax.all_gather(blocks, axes[k], axis=0, tiled=True)  24.9 us
    dot_general x2, matrix products, multiply(): jnp.einsum('stk,skc->stc', tile_block, picked, preferred_element_type=jnp...  19.8 us
    dot_general x2, local copies, waits for them, and re-layouts, multiply(): jnp.einsum('stk,skc->stc', tile_block, picked, preferred_element_type=jnp...  18.8 us
    convert_element_type x2, other arithmetic, multiply(): lower = (products - upper.astype(jnp.float32)).astype(jnp.bfloat16)  8.06 us
    gather x2, local copies, waits for them, and re-layouts, multiply(): picked = jnp.take(blocks, slot_cols, axis=0)  6.05 us
  transfers between devices with their start and end apart: 2, of which 2 were waited for; matrix products, arithmetic and copies ran while one was open for 0% of the time, Pallas kernels for 0%

commit v1 on v0

--- a/solution.py
+++ b/solution.py
@@ -17,7 +17,9 @@
 def gather_in_order(array, axes, order):
     blocks = array[None]
     for k in order:
-        blocks = lax.all_gather(blocks, axes[k], axis=0, tiled=True)
+        blocks = jnp.concatenate(
+            lax.all_to_all(jnp.stack([blocks] * lax.axis_size(axes[k])), axes[k], 0, 0), axis=0
+        )
     held = [lax.axis_size(axes[k]) for k in reversed(order)]
     blocks = blocks.reshape(*held, *array.shape)
     turned = sorted(range(len(order)), key=lambda place: order[len(order) - 1 - place])

time: 297 us -> 341 us (1.15)
  blocking collectives: 119 us -> 187 us
  waiting for transfers between devices: 96.8 us -> 74.2 us
  between operations: 13.5 us -> 0.16 us
  starting transfers between devices: 0.04 us -> 11 us
    all_to_all x0 -> x3, blocking collectives: none -> 96.9 us  [gather_in_order(): lax.all_to_all(jnp.stack([blocks] * lax.axis_size(axes[k])), axes[k], 0, 0)]
    all_gather x2 -> x0, waiting for transfers between devices: 96.8 us -> none  [gather_in_order(): blocks = lax.all_gather(blocks, axes[k], axis=0, tiled=True)]
    all_to_all x0 -> x1, waiting for transfers between devices: none -> 74.2 us  [gather_in_order(): lax.all_to_all(jnp.stack([blocks] * lax.axis_size(axes[k])), axes[k], 0, 0)]
    all_gather x2 -> x0, blocking collectives: 24.9 us -> none  [gather_in_order(): blocks = lax.all_gather(blocks, axes[k], axis=0, tiled=True)]
    all_to_all x0 -> x1, starting transfers between devices: none -> 11 us  [gather_in_order(): lax.all_to_all(jnp.stack([blocks] * lax.axis_size(axes[k])), axes[k], 0, 0)]
    transpose x2 -> x0, local copies, waits for them, and re-layouts: 4.19 us -> none  [gather_in_order(): blocks.transpose(*turned, *range(len(order), blocks.ndim))]
    another operation x0 -> x4, local copies, waits for them, and re-layouts: none -> 4.12 us  [gather_in_order(): jnp.stack([blocks] * lax.axis_size(axes[k]))]
    all_to_all x2, blocking collectives: 94 us -> 90.5 us  [summed_on_arrival(): lax.all_to_all(blocks, axis, split_axis=0, concat_axis=0, tiled=True)]
  transfers between devices with their start and end apart: 2 -> 1, of which waited for: 2 -> 1; matrix products, arithmetic and copies ran while one was open for 0% -> 0% of each run, Pallas kernels for 0% -> 0%
where the time goes in v1:
time: 341 us
  blocking collectives  187 us (55%)
  waiting for transfers between devices  74.2 us (22%)
  local copies, waits for them, and re-layouts  32.9 us (10%)
  matrix products  26 us (8%)
  starting transfers between devices  11 us (3%)
  other arithmetic  9.19 us (3%)
    all_to_all x3, blocking collectives, gather_in_order(): lax.all_to_all(jnp.stack([blocks] * lax.axis_size(axes[k])), axes[k], 0, 0)  96.9 us
    all_to_all x2, blocking collectives, summed_on_arrival(): lax.all_to_all(blocks, axis, split_axis=0, concat_axis=0, tiled=True)  90.5 us
    all_to_all x1, waiting for transfers between devices, gather_in_order(): lax.all_to_all(jnp.stack([blocks] * lax.axis_size(axes[k])), axes[k], 0, 0)  74.2 us
    dot_general x2, matrix products, multiply(): jnp.einsum('stk,skc->stc', tile_block, picked, preferred_element_type=jnp...  19.8 us
    dot_general x2, local copies, waits for them, and re-layouts, multiply(): jnp.einsum('stk,skc->stc', tile_block, picked, preferred_element_type=jnp...  18.8 us
    all_to_all x1, starting transfers between devices, gather_in_order(): lax.all_to_all(jnp.stack([blocks] * lax.axis_size(axes[k])), axes[k], 0, 0)  11 us
    convert_element_type x2, other arithmetic, multiply(): lower = (products - upper.astype(jnp.float32)).astype(jnp.bfloat16)  8.06 us
  transfers between devices with their start and end apart: 1, of which 1 were waited for; matrix products, arithmetic and copies ran while one was open for 0% of the time, Pallas kernels for 0%

profile of v1, /device:TPU:1, one launch (start us, length us, event | category | flops | bytes accessed | tf_op | source)
XLA Modules:
  0.0 340.9 jit_solution(12777028379245012052)
XLA Ops:
  0.0 0.9 stack.12
  0.9 10.9 %all_to_all.30 = bf16[4,1,384,128]{3,2,1,0:T(8,128)(2,1)S(1)} all-to-all(bf16[4,1,384,128]{3,2,1,0:T(8,128)(2,1)S(1)} %stack.12), channel_id=1, replica_groups=mesh['row'=16,'col_0'=4,'col_1'=8] {'col_0'}, dimensions={0} | all-to-all | bytes 786432 | tf_op jit(solution)/shard_map/all_to_all | solution.py:21
  11.8 0.0 copy-start.2
  11.8 2.4 stack.13
  14.2 11.0 %all-to-all-start.1 = ((bf16[8,4,384,128]{3,2,1,0:T(8,128)(2,1)}), bf16[8,4,384,128]{3,2,1,0:T(8,128)(2,1)}, u32[]{:S(2)}, u32[]{:S(2)}) async-start(bf16[8,4,384,128]{3,2,1,0:T(8,128)(2,1)} %stack.13), calls=%async_computation.1 | async-start | bytes 6291456 | tf_op jit(solution)/shard_map/all_to_all | solution.py:21
  25.2 0.0 copy-done.2
  25.2 74.2 %all-to-all-done.1 = bf16[8,4,384,128]{3,2,1,0:T(8,128)(2,1)} async-done(((bf16[8,4,384,128]{3,2,1,0:T(8,128)(2,1)}), bf16[8,4,384,128]{3,2,1,0:T(8,128)(2,1)}, u32[]{:S(2)}, u32[]{:S(2)}) %all-to-all-start.1) | async-done | bytes 3145760 | tf_op jit(solution)/shard_map/all_to_all | solution.py:21
  99.5 2.1 copy.9
  101.6 3.0 gather_fusion
  104.6 9.9 %fusion.12 = f32[128,128,128]{1,2,0:T(8,128)} fusion(bf16[1,1,128,128,128]{4,3,2,1,0:T(8,128)(2,1)} %param.7, bf16[128,128,128]{2,1,0:T(8,128)(2,1)} %gather_fusion, pred[128]{0:T(512)(128)(4,1)S(1)} %compare_and_fusion), kind=kOutput, calls=%fused_computation.20 | convolution fusion | flops 538968064 | bytes 16777344 | tf_op jit(solution)/shard_map/stk,skc->stc/dot_general | solution.py:53
  114.5 9.4 %copy.11 = f32[128,128,128]{0,2,1:T(8,128)} copy(f32[128,128,128]{1,2,0:T(8,128)} %fusion.12) | data formatting | bytes 16777216 | tf_op jit(solution)/shard_map/stk,skc->stc/dot_general | solution.py:53
  123.9 0.0 copy-start.1
  123.9 4.0 %fusion.3 = (bf16[128,16384]{0,1:T(8,128)(2,1)S(1)}, bf16[128,16384]{0,1:T(8,128)(2,1)S(1)}) fusion(f32[128,128,128]{0,2,1:T(8,128)} %copy.11), kind=kLoop, calls=%fused_computation.11 | loop fusion | flops 8388608 | bytes 16777216 | tf_op jit(solution)/shard_map/convert_element_type | solution.py:56
  128.0 0.0 copy-done.1
  128.0 1.5 fusion.25
  129.5 1.5 fusion
  131.1 0.8 convert_element_type.59
  131.9 47.2 %all_to_all.31 = bf16[16,384,128]{2,1,0:T(8,128)(2,1)S(1)} all-to-all(bf16[16,384,128]{2,1,0:T(8,128)(2,1)S(1)} %convert_element_type.59), channel_id=1, replica_groups=mesh['row'=16,'col_0'=4,'col_1'=8] {'row'}, dimensions={0} | all-to-all | bytes 3145728 | tf_op jit(solution)/shard_map/all_to_all | solution.py:41
  179.1 0.2 reduce_sum.24
  179.3 0.1 stack.14
  179.4 10.0 %all_to_all.32 = bf16[4,1,384,128]{3,2,1,0:T(8,128)(2,1)S(1)} all-to-all(bf16[4,1,384,128]{3,2,1,0:T(8,128)(2,1)S(1)} %stack.14), channel_id=1, replica_groups=mesh['row'=16,'col_0'=4,'col_1'=8] {'col_0'}, dimensions={0} | all-to-all | bytes 786432 | tf_op jit(solution)/shard_map/all_to_all | solution.py:21
  189.4 0.7 stack.15
  190.1 76.0 %all_to_all.33 = bf16[8,4,384,128]{3,2,1,0:T(8,128)(2,1)S(1)} all-to-all(bf16[8,4,384,128]{3,2,1,0:T(8,128)(2,1)S(1)} %stack.15), channel_id=1, replica_groups=mesh['row'=16,'col_0'=4,'col_1'=8] {'col_1'}, dimensions={0} | all-to-all | bytes 6291456 | tf_op jit(solution)/shard_map/all_to_all | solution.py:21
  266.2 0.2 copy.12
  266.4 3.0 gather_fusion.1
  269.4 9.9 %fusion.17 = f32[128,128,128]{1,2,0:T(8,128)} fusion(bf16[1,1,128,128,128]{4,3,2,1,0:T(8,128)(2,1)} %param.7, bf16[128,128,128]{2,1,0:T(8,128)(2,1)} %gather_fusion.1, pred[128]{0:T(512)(128)(4,1)S(1)} %compare_and_fusion), kind=kOutput, calls=%fused_computation.21 | convolution fusion | flops 538968064 | bytes 16777344 | tf_op jit(solution)/shard_map/stk,skc->stc/dot_general | solution.py:53
  279.3 9.4 %copy.14 = f32[128,128,128]{0,2,1:T(8,128)} copy(f32[128,128,128]{1,2,0:T(8,128)} %fusion.17) | data formatting | bytes 16777216 | tf_op jit(solution)/shard_map/stk,skc->stc/dot_general | solution.py:53
  288.7 4.0 %fusion.2 = (bf16[128,16384]{0,1:T(8,128)(2,1)S(1)}, bf16[128,16384]{0,1:T(8,128)(2,1)S(1)}) fusion(f32[128,128,128]{0,2,1:T(8,128)} %copy.14), kind=kLoop, calls=%fused_computation.8 | loop fusion | flops 8388608 | bytes 16777216 | tf_op jit(solution)/shard_map/convert_element_type | solution.py:56
  292.8 1.5 fusion.24
  294.3 1.5 fusion.1
  295.9 0.0 copy-start
  295.9 0.8 convert_element_type.65
  296.7 43.3 %all_to_all.34 = bf16[16,384,128]{2,1,0:T(8,128)(2,1)S(1)} all-to-all(bf16[16,384,128]{2,1,0:T(8,128)(2,1)S(1)} %convert_element_type.65), channel_id=1, replica_groups=mesh['row'=16,'col_0'=4,'col_1'=8] {'row'}, dimensions={0} | all-to-all | bytes 3145728 | tf_op jit(solution)/shard_map/all_to_all | solution.py:41
  340.0 0.2 reduce_sum.25
  340.2 0.0 copy-done
  340.2 0.7 add_convert_fusion
  (3 shorter events, 0.0 us)
Async XLA Ops:
  11.8 13.4 %copy-start.2 = (s32[1,1,128]{2,1,0:T(1,128)S(1)}, s32[1,1,128]{2,1,0:T(1,128)}, u32[]{:S(2)}) copy-start(s32[1,1,128]{2,1,0:T(1,128)} %param.9) | copy-start | bytes 1540
  14.2 85.2 %all-to-all-start.1 = ((bf16[8,4,384,128]{3,2,1,0:T(8,128)(2,1)}), bf16[8,4,384,128]{3,2,1,0:T(8,128)(2,1)}, u32[]{:S(2)}, u32[]{:S(2)}) async-start(bf16[8,4,384,128]{3,2,1,0:T(8,128)(2,1)} %stack.13), calls=%async_computation.1 | async-start | bytes 6291456 | tf_op jit(solution)/shard_map/all_to_all | solution.py:21
  123.9 4.0 %copy-start.1 = (s32[1,1,128]{2,1,0:T(1,128)S(1)}, s32[1,1,128]{2,1,0:T(1,128)}, u32[]{:S(2)}) copy-start(s32[1,1,128]{2,1,0:T(1,128)} %param.8) | copy-start | bytes 1540
  295.9 44.3 %copy-start = (bf16[384,128]{1,0:T(8,128)(2,1)S(1)}, bf16[384,128]{1,0:T(8,128)(2,1)}, u32[]{:S(2)}) copy-start(bf16[384,128]{1,0:T(8,128)(2,1)} %param.6) | copy-start | bytes 294916
